TPU v7x, 32 devices: a whole 2x2x4 slice. The times are simulated.
32 devices in a mesh: segment: 4 (over z), ctx: 4 (over y, x), tp: 2 (over core).
Axes of the slice: x: 2, y: 2, z: 4, core: 2. Of those that a mesh axis runs over, the one named last changes fastest.
Arguments:
- queries: bfloat16 [4, 512, 8, 640], P('segment', 'ctx', 'tp'), may hold values from -200 to 200
- pairs: bfloat16 [4, 512, 8, 256], P('segment', 'ctx', 'tp'), may hold values from -6 to 6
- out_proj: bfloat16 [4, 8, 640, 5120], P('segment', 'tp'), may hold values from -0.625 to 0.625
- lengths: int32 [4, 4], replicated, may hold values from 1 to 256, 512 in all within a row
Outputs:
- scored: bfloat16 [4, 512, 5120], P('segment', 'ctx', 'tp')
Inputs may be any that keep to these rules, and one draw needn't show every extreme that they name: `lengths`: each row sums to 512; its largest length is exactly 256.
All inputs are finite; a program needn't handle non-finite values.
Results may differ from a plain program's by a relative error of at most 0.014.
Values may be sent and summed in bfloat16 or wider, within the bound.
A program may use at most 64 MiB of HBM per device.

v0:
```python
import math
import jax
import jax.numpy as jnp
from jax import lax
from jax.sharding import PartitionSpec as P


def from_behind(value, axis, by):
    size = lax.axis_size(axis)
    return lax.ppermute(value, axis, [(i, (i + by) % size) for i in range(size)])


def rollout_ids(positions, row_lengths):
    row_ends = jnp.cumsum(row_lengths)
    return jnp.sum((positions[:, None] >= row_ends[None, :]).astype(jnp.int32), axis=1)


def attend(query_shard, pair_shard, row_lengths):
    rows_here = query_shard.shape[1]
    local_heads = pair_shard.shape[2]
    head_dim = pair_shard.shape[3] // 2
    group_size = query_shard.shape[3] // head_dim
    first_pos = lax.axis_index("ctx") * rows_here
    query_pos = first_pos + jnp.arange(rows_here, dtype=jnp.int32)
    query_rollout = rollout_ids(query_pos, row_lengths)
    query_heads = query_shard[0].reshape(rows_here, local_heads, group_size, head_dim)
    score_scale = 1.0 / math.sqrt(head_dim)

    def update(state_in, key_block, key_begin):
        running_max, denom, accum = state_in
        block_len = key_block.shape[0]
        key_pos = key_begin + jnp.arange(block_len, dtype=jnp.int32)
        key_rollout = rollout_ids(key_pos, row_lengths)
        visible = (query_rollout[:, None] == key_rollout[None, :]) & (
            key_pos[None, :] <= query_pos[:, None]
        )
        scores = (
            jnp.einsum(
                "rhgd,khd->hgrk",
                query_heads,
                key_block[:, :, :head_dim],
                preferred_element_type=jnp.float32,
            )
            * score_scale
        )
        scores = jnp.where(visible, scores, -1e30)
        new_max = jnp.maximum(running_max, jnp.max(scores, axis=-1))
        rescale = jnp.exp(running_max - new_max)
        weights = jnp.where(visible, jnp.exp(scores - new_max[..., None]), 0.0)
        denom = denom * rescale + jnp.sum(weights, axis=-1)
        added = jnp.einsum(
            "hgrk,khd->hgrd",
            weights.astype(jnp.bfloat16),
            key_block[:, :, head_dim:],
            preferred_element_type=jnp.float32,
        )
        accum = accum * rescale[..., None] + added
        return (new_max, denom, accum)

    starting = (
        jnp.full((local_heads, group_size, rows_here), -1e30, jnp.float32),
        jnp.zeros((local_heads, group_size, rows_here), jnp.float32),
        jnp.zeros((local_heads, group_size, rows_here, head_dim), jnp.float32),
    )
    shards = lax.all_gather(pair_shard[0], "ctx", axis=0, tiled=True)
    shard_rows = shards.shape[0]
    block_len = math.gcd(shard_rows, 512)

    def one_step(step_index, inner):
        key_block = lax.dynamic_slice_in_dim(shards, step_index * block_len, block_len, 0)
        return update(inner, key_block, step_index * block_len)

    running_max, denom, accum = lax.fori_loop(0, shard_rows // block_len, one_step, starting)
    outputs = accum / denom[..., None]
    outputs = jnp.transpose(outputs, (2, 0, 1, 3)).reshape(
        1, rows_here, local_heads, group_size * head_dim
    )
    return outputs.astype(jnp.bfloat16)


def local(queries, pairs, out_proj, lengths):
    section = lax.axis_index("segment")
    own_result = attend(queries, pairs, lengths[section])
    attended = from_behind(own_result, "segment", -1)
    rows_here = attended.shape[1]
    partial_sum = jnp.dot(
        attended.reshape(rows_here, -1),
        out_proj[0].reshape(-1, out_proj.shape[3]),
        preferred_element_type=jnp.float32,
    )
    shares = lax.psum_scatter(
        partial_sum.astype(jnp.bfloat16), "tp", scatter_dimension=1, tiled=True
    )
    return shares.reshape(1, rows_here, -1)


def solution(mesh):
    return jax.shard_map(
        local,
        mesh=mesh,
        in_specs=(
            P("segment", "ctx", "tp", None),
            P("segment", "ctx", "tp", None),
            P("segment", "tp", None, None),
            P(),
        ),
        out_specs=P("segment", "ctx", "tp"),
        check_vma=False,
    )
```

profile of v0, /device:TPU:0, one launch (start us, length us, event | category | flops | bytes accessed | tf_op | source)
XLA Modules:
  0.0 89.1 jit_solution(15405422814970957084)
XLA Ops:
  6.5 0.0 copy-start
  6.5 0.0 all-gather.3.cloned.1.call-start
  6.5 1.7 %copy.16 = bf16[1,128,4,256]{3,1,2,0:T(8,128)(2,1)} copy(bf16[1,128,4,256]{3,2,1,0:T(4,128)(2,1)} %param.5) | data formatting | bytes 524288 | tf_op args[1]
  8.2 0.0 all-gather.3.cloned.1.call-update
  8.3 0.0 reduce-scatter.2.cloned.1.call-start
  8.3 0.0 copy-done
  8.3 0.2 reduce-window.8
  8.5 1.6 %copy.17 = bf16[1,128,4,640]{1,3,2,0:T(8,128)(2,1)S(1)} copy(bf16[1,128,4,640]{3,2,1,0:T(4,128)(2,1)} %param.4) | data formatting | bytes 1310720 | tf_op args[0]
  10.1 0.1 convert_reduce_fusion
  10.2 0.1 convert_reduce_fusion.1
  10.3 0.1 fusion.24
  10.4 28.0 %all-gather.3.cloned.1.call-done = bf16[1,512,4,256]{3,1,2,0:T(8,128)(2,1)} async-done(((bf16[1,128,4,256]{3,1,2,0:T(8,128)(2,1)}), bf16[1,512,4,256]{3,1,2,0:T(8,128)(2,1)}) %all-gather.3.cloned.1.call-update) | async-done | bytes 1048592 | tf_op jit(solution)/shard_map/all_gather | solution.py:65
  38.4 0.0 copy-start.1
  38.4 2.0 %fusion.8 = (f32[4,5,128]{2,1,0:T(8,128)S(1)}, f32[4,512,128,5]{2,1,3,0:T(8,128)S(1)}) fusion(pred[128,512]{0,1:T(8,128)(4,1)S(1)} %fusion.24, bf16[128,4,5,128]{0,3,2,1:T(8,128)(2,1)S(1)} %bitcast.63, bf16[512,4,256]{2,0,1:T(8,128)(2,1)} %bitcast.65), kind=kOutput, calls=%fused_computation.6 | convolution fusion | flops 339473920 | bytes 6498304 | tf_op jit(solution)/shard_map/while/body/eval_jaxpr/rhgd,khd->hgrk/dot_general | solution.py:38
  40.5 1.3 %fusion.9 = f32[4,5,128]{2,1,0:T(8,128)S(1)} fusion(f32[4,512,128,5]{2,1,3,0:T(8,128)S(1)} %get-tuple-element.26, f32[4,5,128]{2,1,0:T(8,128)S(1)} %get-tuple-element.24, pred[128,512]{0,1:T(8,128)(4,1)S(1)} %fusion.24), kind=kLoop, calls=%fused_computation.7 | loop fusion | flops 6551040 | bytes 5328896 | tf_op jit(solution)/shard_map/while/body/eval_jaxpr/reduce_sum | solution.py:50
  41.8 0.0 copy-done.1
  41.8 1.5 %divide_convert_fusion = bf16[128,4,5,128]{0,3,2,1:T(8,128)(2,1)S(1)} fusion(f32[4,512,128,5]{2,1,3,0:T(8,128)S(1)} %get-tuple-element.26, f32[4,5,128]{2,1,0:T(8,128)S(1)} %get-tuple-element.24, pred[128,512]{0,1:T(8,128)(4,1)S(1)} %fusion.24, f32[128,4,5]{0,2,1:T(8,128)S(1)} %bitcast_add_fusion, f32[128,4,5]{0,2,1:T(8,128)S(1)} %get-tuple-element.23, ...), kind=kOutput, calls=%fused_computation.13 | convolution fusion | flops 343080960 | bytes 6537216 | tf_op jit(solution)/shard_map/while/body/eval_jaxpr/hgrk,khd->hgrd/dot_general | solution.py:51
  43.3 0.3 copy.21
  43.6 3.4 %collective-permute-start = (bf16[1,128,4,640]{3,1,2,0:T(8,128)(2,1)S(1)}, bf16[1,128,4,640]{3,1,2,0:T(8,128)(2,1)S(1)}, u32[]{:S(2)}, u32[]{:S(2)}) collective-permute-start(bf16[1,128,4,640]{3,1,2,0:T(8,128)(2,1)S(1)} %copy.21), channel_id=1, source_target_pairs={{0,24},{8,0},{16,8},{24,16},{1,25},{9,1},{17,9},{25,17},{2,26},{10... | collective-permute-start | bytes 1966088 | tf_op jit(solution)/shard_map/ppermute | solution.py:10
  47.0 13.8 %collective-permute-done = bf16[1,128,4,640]{3,1,2,0:T(8,128)(2,1)S(1)} collective-permute-done((bf16[1,128,4,640]{3,1,2,0:T(8,128)(2,1)S(1)}, bf16[1,128,4,640]{3,1,2,0:T(8,128)(2,1)S(1)}, u32[]{:S(2)}, u32[]{:S(2)}) %collective-permute-start) | collective-permute-done | bytes 655392 | tf_op jit(solution)/shard_map/ppermute | solution.py:10
  60.8 11.7 %fusion.5 = bf16[128,5120]{1,0:T(8,128)(2,1)} fusion(bf16[1,4,640,5120]{3,2,1,0:T(8,128)(2,1)} %param.6, bf16[1,128,4,640]{3,1,2,0:T(8,128)(2,1)S(1)} %collective-permute-done), kind=kOutput, calls=%fused_computation.3 | convolution fusion | flops 3356098560 | bytes 28180480 | tf_op jit(solution)/shard_map/dot_general | solution.py:86
  72.5 0.0 reduce-scatter.2.cloned.1.call-update
  72.6 9.7 %reduce-scatter.2.cloned.1.call-done = bf16[128,2560]{1,0:T(8,128)(2,1)} async-done(((bf16[128,5120]{1,0:T(8,128)(2,1)}), bf16[128,2560]{1,0:T(8,128)(2,1)}) %reduce-scatter.2.cloned.1.call-update) | async-done | bytes 655376 | tf_op jit(solution)/shard_map/reduce_scatter | solution.py:91
  (4 shorter events, 0.0 us)
Async XLA Ops:
  6.5 1.8 %copy-start = (s32[4,4]{1,0:T(4,128)S(1)}, s32[4,4]{1,0:T(4,128)}, u32[]{:S(2)}) copy-start(s32[4,4]{1,0:T(4,128)} %param.7) | copy-start | bytes 196
  6.5 31.9 %all-gather.3.cloned.1.call-start = ((), (), s32[]{:S(2)}) async-start(), calls=%async_computation.2 | async-start | bytes 1310720 | tf_op jit(solution)/shard_map/all_gather | solution.py:65
  8.3 74.0 %reduce-scatter.2.cloned.1.call-start = ((), (), s32[]{:S(2)}) async-start(), calls=%async_computation.1 | async-start | bytes 1966080 | tf_op jit(solution)/shard_map/reduce_scatter | solution.py:91
  38.4 3.3 %copy-start.1 = (bf16[1,512,4,256]{3,1,2,0:T(8,128)(2,1)S(1)}, bf16[1,512,4,256]{3,1,2,0:T(8,128)(2,1)}, u32[]{:S(2)}) copy-start(bf16[1,512,4,256]{3,1,2,0:T(8,128)(2,1)} %all-gather.3.cloned.1.call-done) | copy-start | bytes 3145732
  43.6 17.2 %collective-permute-start = (bf16[1,128,4,640]{3,1,2,0:T(8,128)(2,1)S(1)}, bf16[1,128,4,640]{3,1,2,0:T(8,128)(2,1)S(1)}, u32[]{:S(2)}, u32[]{:S(2)}) collective-permute-start(bf16[1,128,4,640]{3,1,2,0:T(8,128)(2,1)S(1)} %copy.21), channel_id=1, source_target_pairs={{0,24},{8,0},{16,8},{24,16},{1,25},{9,1},{17,9},{25,17},{2,26},{10... | collective-permute-start | bytes 1966088 | tf_op jit(solution)/shard_map/ppermute | solution.py:10
Sparse Core Ops, SparseCore 0:
  9.2 29.2 all-gather.2
  72.7 9.5 reduce-scatter.1
where the time goes:
time: 89.3 us; the launch traced here: 89.1 us
  waiting for transfers between devices  51.6 us (58%)
  matrix products  15.2 us (17%)
  between operations  13.5 us (15%)
  local copies, waits for them, and re-layouts  3.62 us (4%)
  starting transfers between devices  3.43 us (4%)
  other arithmetic  1.76 us (2%)
    all_gather x1, waiting for transfers between devices, attend(): shards = lax.all_gather(pair_shard[0], 'ctx', axis=0, tiled=True)  28 us
    ppermute x1, waiting for transfers between devices, from_behind(): lax.ppermute(value, axis, [(i, (i + by) % size) for i in range(size)])  13.8 us
    dot_general x1, matrix products, local(): jnp.dot(attended.reshape(rows_here, -1), out_proj[0].reshape(-1, out_proj...  11.7 us
    reduce_scatter x1, waiting for transfers between devices, local(): lax.psum_scatter(partial_sum.astype(jnp.bfloat16), 'tp', scatter_dimensio...  9.74 us
    ppermute x1, starting transfers between devices, from_behind(): lax.ppermute(value, axis, [(i, (i + by) % size) for i in range(size)])  3.38 us
    unnamed x6, local copies, waits for them, and re-layouts  3.29 us
    dot_general x1, matrix products, update(): jnp.einsum('rhgd,khd->hgrk', query_heads, key_block[:, :, :head_dim], pre...  2.02 us
  transfers between devices with their start and end apart: 3, of which 3 were waited for; matrix products, arithmetic and copies ran while one was open for 2% of the time, Pallas kernels for 0%

commit v1 on v0

--- a/solution.py
+++ b/solution.py
@@ -1,8 +1,25 @@
+import functools
 import math
 import jax
 import jax.numpy as jnp
 from jax import lax
 from jax.sharding import PartitionSpec as P
+
+
+def put_rings_on(array_in, along_axis, d_out):
+    axis_n = jax.lax.axis_size(along_axis)
+    x_next = [None] * axis_n
+    cards = list(map(lambda u: (u, (u + 1) % axis_n), range(axis_n)))
+    x_next[axis_n - 1] = array_in
+    for k in range(axis_n - 2, -1, -1):
+        x_next[k] = jax.lax.ppermute(x_next[k + 1], along_axis, cards)
+    known = jnp.concatenate(x_next, axis=d_out)
+    return jnp.roll(
+        known, shift=(jax.lax.axis_index(along_axis) + 1) * array_in.shape[d_out], axis=d_out
+    )
+
+
+_save_turns = functools.partial(put_rings_on, along_axis="ctx", d_out=0)
 
 
 def from_behind(value, axis, by):
@@ -62,7 +79,7 @@
         jnp.zeros((local_heads, group_size, rows_here), jnp.float32),
         jnp.zeros((local_heads, group_size, rows_here, head_dim), jnp.float32),
     )
-    shards = lax.all_gather(pair_shard[0], "ctx", axis=0, tiled=True)
+    shards = _save_turns(pair_shard[0])
     shard_rows = shards.shape[0]
     block_len = math.gcd(shard_rows, 512)
 

time: 89.3 us -> 81 us (0.907)
  waiting for transfers between devices: 51.6 us -> 41.2 us
  starting transfers between devices: 3.43 us -> 7.13 us
  matrix products: 15.2 us -> 14.1 us
    all_gather x1 -> x0, waiting for transfers between devices: 28 us -> none  [attend(): shards = lax.all_gather(pair_shard[0], 'ctx', axis=0, tiled=True)]
    ppermute x0 -> x3, waiting for transfers between devices: none -> 20.2 us  [put_rings_on(): x_next[k] = jax.lax.ppermute(x_next[k + 1], along_axis, cards)]
    ppermute x0 -> x3, starting transfers between devices: none -> 3.81 us  [put_rings_on(): x_next[k] = jax.lax.ppermute(x_next[k + 1], along_axis, cards)]
    ppermute x1, waiting for transfers between devices: 13.8 us -> 11.1 us  [from_behind(): lax.ppermute(value, axis, [(i, (i + by) % size) for i in range(size)])]
    dot_general x1, matrix products: 2.02 us -> 0.92 us  [update(): jnp.einsum('rhgd,khd->hgrk', query_heads, key_block[:, :, :head_dim], pre...]
    unnamed x6 -> x13, local copies, waits for them, and re-layouts: 3.29 us -> 2.8 us
  transfers between devices with their start and end apart: 3 -> 5, of which waited for: 3 -> 5; matrix products, arithmetic and copies ran while one was open for 2% -> 3% of each run, Pallas kernels for 0% -> 0%
where the time goes in v1:
time: 81 us; the launch traced here: 80.9 us
  waiting for transfers between devices  41.2 us (51%)
  matrix products  14.1 us (17%)
  between operations  13.5 us (17%)
  starting transfers between devices  7.13 us (9%)
  local copies, waits for them, and re-layouts  3.15 us (4%)
  other arithmetic  1.76 us (2%)
    ppermute x3, waiting for transfers between devices, put_rings_on(): x_next[k] = jax.lax.ppermute(x_next[k + 1], along_axis, cards)  20.2 us
    dot_general x1, matrix products, local(): jnp.dot(attended.reshape(rows_here, -1), out_proj[0].reshape(-1, out_proj...  11.7 us
    ppermute x1, waiting for transfers between devices, from_behind(): lax.ppermute(value, axis, [(i, (i + by) % size) for i in range(size)])  11.1 us
    reduce_scatter x1, waiting for transfers between devices, local(): lax.psum_scatter(partial_sum.astype(jnp.bfloat16), 'tp', scatter_dimensio...  9.8 us
    ppermute x3, starting transfers between devices, put_rings_on(): x_next[k] = jax.lax.ppermute(x_next[k + 1], along_axis, cards)  3.81 us
    ppermute x1, starting transfers between devices, from_behind(): lax.ppermute(value, axis, [(i, (i + by) % size) for i in range(size)])  3.33 us
    unnamed x13, local copies, waits for them, and re-layouts  2.8 us
  transfers between devices with their start and end apart: 5, of which 5 were waited for; matrix products, arithmetic and copies ran while one was open for 3% of the time, Pallas kernels for 0%

profile of v1, /device:TPU:0, one launch (start us, length us, event | category | flops | bytes accessed | tf_op | source)
XLA Modules:
  0.0 80.9 jit_solution(18145054620688694647)
XLA Ops:
  6.5 0.0 copy-start
  6.5 0.0 copy-start.1
  6.5 0.0 reduce-scatter.2.cloned.1.call-start
  6.5 1.0 %copy.33 = bf16[1,128,4,256]{3,1,2,0:T(8,128)(2,1)S(1)} copy(bf16[1,128,4,256]{3,2,1,0:T(4,128)(2,1)} %param.5) | data formatting | bytes 524288 | tf_op args[1]
  7.6 3.0 %collective-permute-start = (bf16[128,4,256]{2,0,1:T(8,128)(2,1)S(1)}, bf16[128,4,256]{2,0,1:T(8,128)(2,1)S(1)}, u32[]{:S(2)}, u32[]{:S(2)}) collective-permute-start(bf16[128,4,256]{2,0,1:T(8,128)(2,1)S(1)} %bitcast.71), channel_id=1, source_target_pairs={{0,2},{2,4},{4,6},{6,0},{1,3},{3,5},{5,7},{7,1},{8,10},{10,12},{12... | collective-permute-start | bytes 786440 | tf_op jit(solution)/shard_map/ppermute | solution.py:15
  10.6 7.3 %collective-permute-done = bf16[128,4,256]{2,0,1:T(8,128)(2,1)S(1)} collective-permute-done((bf16[128,4,256]{2,0,1:T(8,128)(2,1)S(1)}, bf16[128,4,256]{2,0,1:T(8,128)(2,1)S(1)}, u32[]{:S(2)}, u32[]{:S(2)}) %collective-permute-start) | collective-permute-done | bytes 262176 | tf_op jit(solution)/shard_map/ppermute | solution.py:15
  17.9 0.8 collective-permute-start.1
  18.7 0.0 copy-done
  18.7 0.2 reduce-window.8
  18.9 0.1 convert_reduce_fusion.1
  18.9 7.3 %collective-permute-done.1 = bf16[128,4,256]{2,0,1:T(8,128)(2,1)S(1)} collective-permute-done((bf16[128,4,256]{2,0,1:T(8,128)(2,1)S(1)}, bf16[128,4,256]{2,0,1:T(8,128)(2,1)S(1)}, u32[]{:S(2)}, u32[]{:S(2)}) %collective-permute-start.1) | collective-permute-done | bytes 262176 | tf_op jit(solution)/shard_map/ppermute | solution.py:15
  26.2 0.0 collective-permute-start.2
  26.2 0.1 convert_reduce_fusion
  26.3 1.6 %copy.17 = bf16[1,128,4,640]{1,3,2,0:T(8,128)(2,1)S(1)} copy(bf16[1,128,4,640]{3,2,1,0:T(4,128)(2,1)} %param.4) | data formatting | bytes 1310720 | tf_op args[0]
  27.9 0.1 fusion.24
  28.1 5.7 %collective-permute-done.2 = bf16[128,4,256]{2,0,1:T(8,128)(2,1)S(1)} collective-permute-done((bf16[128,4,256]{2,0,1:T(8,128)(2,1)S(1)}, bf16[128,4,256]{2,0,1:T(8,128)(2,1)S(1)}, u32[]{:S(2)}, u32[]{:S(2)}) %collective-permute-start.2) | collective-permute-done | bytes 262176 | tf_op jit(solution)/shard_map/ppermute | solution.py:15
  33.8 0.0 copy-done.1
  34.0 0.9 %fusion.8 = (f32[4,5,128]{2,1,0:T(8,128)S(1)}, f32[4,512,128,5]{2,1,3,0:T(8,128)S(1)}) fusion(pred[128,512]{0,1:T(8,128)(4,1)S(1)} %fusion.24, bf16[128,4,5,128]{0,3,2,1:T(8,128)(2,1)S(1)} %bitcast.69, bf16[1024,4,256]{2,0,1:T(8,128)(2,1)S(1)} %constant_dynamic-update-slice_fusion, s32[]{:T(128)S(6)} %select_n.29), kind=kOutput, calls=%fused_computation.6 | convolution fusion | flops 339473920 | bytes 6498308 | tf_op jit(solution)/shard_map/while/body/eval_jaxpr/rhgd,khd->hgrk/dot_general | solution.py:55
  34.9 1.2 %fusion.9 = f32[4,5,128]{2,1,0:T(8,128)S(1)} fusion(f32[4,512,128,5]{2,1,3,0:T(8,128)S(1)} %get-tuple-element.26, f32[4,5,128]{2,1,0:T(8,128)S(1)} %get-tuple-element.24, pred[128,512]{0,1:T(8,128)(4,1)S(1)} %fusion.24), kind=kLoop, calls=%fused_computation.7 | loop fusion | flops 6551040 | bytes 5328896 | tf_op jit(solution)/shard_map/while/body/eval_jaxpr/reduce_sum | solution.py:67
  36.2 1.5 %divide_convert_fusion = bf16[128,4,5,128]{0,3,2,1:T(8,128)(2,1)S(1)} fusion(f32[4,512,128,5]{2,1,3,0:T(8,128)S(1)} %get-tuple-element.26, f32[4,5,128]{2,1,0:T(8,128)S(1)} %get-tuple-element.24, pred[128,512]{0,1:T(8,128)(4,1)S(1)} %fusion.24, f32[128,4,5]{0,2,1:T(8,128)S(1)} %bitcast_add_fusion, f32[128,4,5]{0,2,1:T(8,128)S(1)} %get-tuple-element.23, ...), kind=kOutput, calls=%fused_computation.13 | convolution fusion | flops 343080960 | bytes 6537224 | tf_op jit(solution)/shard_map/while/body/eval_jaxpr/hgrk,khd->hgrd/dot_general | solution.py:68
  37.7 0.3 copy.21
  38.0 3.3 %collective-permute-start.3 = (bf16[1,128,4,640]{3,1,2,0:T(8,128)(2,1)S(1)}, bf16[1,128,4,640]{3,1,2,0:T(8,128)(2,1)S(1)}, u32[]{:S(2)}, u32[]{:S(2)}) collective-permute-start(bf16[1,128,4,640]{3,1,2,0:T(8,128)(2,1)S(1)} %copy.21), channel_id=1, source_target_pairs={{0,24},{8,0},{16,8},{24,16},{1,25},{9,1},{17,9},{25,17},{2,26},{10... | collective-permute-start | bytes 1966088 | tf_op jit(solution)/shard_map/ppermute | solution.py:27
  41.4 11.1 %collective-permute-done.3 = bf16[1,128,4,640]{3,1,2,0:T(8,128)(2,1)S(1)} collective-permute-done((bf16[1,128,4,640]{3,1,2,0:T(8,128)(2,1)S(1)}, bf16[1,128,4,640]{3,1,2,0:T(8,128)(2,1)S(1)}, u32[]{:S(2)}, u32[]{:S(2)}) %collective-permute-start.3) | collective-permute-done | bytes 655392 | tf_op jit(solution)/shard_map/ppermute | solution.py:27
  52.5 11.7 %fusion.5 = bf16[128,5120]{1,0:T(8,128)(2,1)} fusion(bf16[1,4,640,5120]{3,2,1,0:T(8,128)(2,1)} %param.6, bf16[1,128,4,640]{3,1,2,0:T(8,128)(2,1)S(1)} %collective-permute-done.3), kind=kOutput, calls=%fused_computation.3 | convolution fusion | flops 3356098560 | bytes 28180480 | tf_op jit(solution)/shard_map/dot_general | solution.py:103
  64.2 0.0 reduce-scatter.2.cloned.1.call-update
  64.3 9.8 %reduce-scatter.2.cloned.1.call-done = bf16[128,2560]{1,0:T(8,128)(2,1)} async-done(((bf16[128,5120]{1,0:T(8,128)(2,1)}), bf16[128,2560]{1,0:T(8,128)(2,1)}) %reduce-scatter.2.cloned.1.call-update) | async-done | bytes 655376 | tf_op jit(solution)/shard_map/reduce_scatter | solution.py:108
  (12 shorter events, 0.2 us)
Async XLA Ops:
  6.5 12.1 %copy-start = (s32[4,4]{1,0:T(4,128)S(1)}, s32[4,4]{1,0:T(4,128)}, u32[]{:S(2)}) copy-start(s32[4,4]{1,0:T(4,128)} %param.7) | copy-start | bytes 196
  6.5 27.3 %copy-start.1 = (bf16[1,128,4,256]{3,2,1,0:T(4,128)(2,1)S(1)}, bf16[1,128,4,256]{3,2,1,0:T(4,128)(2,1)}, u32[]{:S(2)}) copy-start(bf16[1,128,4,256]{3,2,1,0:T(4,128)(2,1)} %param.5) | copy-start | bytes 786436
  6.5 67.5 %reduce-scatter.2.cloned.1.call-start = ((), (), s32[]{:S(2)}) async-start(), calls=%async_computation.1 | async-start | bytes 1966080 | tf_op jit(solution)/shard_map/reduce_scatter | solution.py:108
  7.6 10.3 %collective-permute-start = (bf16[128,4,256]{2,0,1:T(8,128)(2,1)S(1)}, bf16[128,4,256]{2,0,1:T(8,128)(2,1)S(1)}, u32[]{:S(2)}, u32[]{:S(2)}) collective-permute-start(bf16[128,4,256]{2,0,1:T(8,128)(2,1)S(1)} %bitcast.71), channel_id=1, source_target_pairs={{0,2},{2,4},{4,6},{6,0},{1,3},{3,5},{5,7},{7,1},{8,10},{10,12},{12... | collective-permute-start | bytes 786440 | tf_op jit(solution)/shard_map/ppermute | solution.py:15
  17.9 8.4 %collective-permute-start.1 = (bf16[128,4,256]{2,0,1:T(8,128)(2,1)S(1)}, bf16[128,4,256]{2,0,1:T(8,128)(2,1)S(1)}, u32[]{:S(2)}, u32[]{:S(2)}) collective-permute-start(bf16[128,4,256]{2,0,1:T(8,128)(2,1)S(1)} %collective-permute-done), channel_id=1, source_target_pairs={{0,2},{2,4},{4,6},{6,0},{1,3},{3,5},{5,7},{7,1},{8,10},{10,12},{12... | collective-permute-start | bytes 786440 | tf_op jit(solution)/shard_map/ppermute | solution.py:15
  26.2 7.5 %collective-permute-start.2 = (bf16[128,4,256]{2,0,1:T(8,128)(2,1)S(1)}, bf16[128,4,256]{2,0,1:T(8,128)(2,1)S(1)}, u32[]{:S(2)}, u32[]{:S(2)}) collective-permute-start(bf16[128,4,256]{2,0,1:T(8,128)(2,1)S(1)} %collective-permute-done.1), channel_id=1, source_target_pairs={{0,2},{2,4},{4,6},{6,0},{1,3},{3,5},{5,7},{7,1},{8,10},{10,12},{12... | collective-permute-start | bytes 786440 | tf_op jit(solution)/shard_map/ppermute | solution.py:15
  38.0 14.5 %collective-permute-start.3 = (bf16[1,128,4,640]{3,1,2,0:T(8,128)(2,1)S(1)}, bf16[1,128,4,640]{3,1,2,0:T(8,128)(2,1)S(1)}, u32[]{:S(2)}, u32[]{:S(2)}) collective-permute-start(bf16[1,128,4,640]{3,1,2,0:T(8,128)(2,1)S(1)} %copy.21), channel_id=1, source_target_pairs={{0,24},{8,0},{16,8},{24,16},{1,25},{9,1},{17,9},{25,17},{2,26},{10... | collective-permute-start | bytes 1966088 | tf_op jit(solution)/shard_map/ppermute | solution.py:27
Sparse Core Ops, SparseCore 0:
  64.4 9.6 reduce-scatter.1
